TPU v7x, 256 devices: a whole 4x4x8 slice. The times are simulated.
256 devices in a mesh: shot: 32 (over y_hi, z, core), rcv: 8 (over x, y_lo).
Axes of the slice: x: 4, y: 4 (y_hi: 2, y_lo: 2; y = y_hi * 2 + y_lo), z: 8, core: 2. Of those that a mesh axis runs over, the one named last changes fastest.
Arguments:
- record: bfloat16 [768, 262144], P('rcv', 'shot'), may hold values from -6 to 6
- shot_fire_samples: int32 [1024], P('shot'), may hold values from 0 to 262143, as said below
Outputs:
- psf_gram: float32 [2, 4, 768, 768], P(None, None, 'rcv', 'shot')
Inputs may be any that keep to these rules, and one draw needn't show every extreme that they name: `shot_fire_samples`: shot s fires at a sample from s * 256 to s * 256 + 255.
All inputs are finite; a program needn't handle non-finite values.
Results may differ from a plain program's by a relative error of at most 0.0025.
Values may be sent and summed in bfloat16 or wider, within the bound.
No kernel may reach another device: no remote copies, remote signals or barrier semaphores. Data moves between devices by JAX's collectives and lax.ppermute only.
A program may use at most 64 MiB of HBM per device.

v0:
```python
import math
import jax
import jax.numpy as jnp
from jax import lax
from jax.sharding import PartitionSpec as P

WIN = 2048
SPACING = 256
freq_bins = (24, 40, 56, 80)


def shifted(block, axis, distance):
    devices = range(lax.axis_size(axis))
    route = [(i - distance, i) for i in devices if i - distance in devices]
    return lax.ppermute(block, axis, route)


def dft_table(window_len):
    lag_index = jnp.arange(window_len, dtype=jnp.int32)
    bin_list = jnp.array(freq_bins, dtype=jnp.int32)
    turn_count = lag_index[:, None] * bin_list[None, :] % window_len
    phase_angle = 2.0 * math.pi / window_len * turn_count.astype(jnp.float32)
    dft_rows = jnp.concatenate([jnp.cos(phase_angle), -jnp.sin(phase_angle)], axis=1) / math.sqrt(
        window_len
    )
    return dft_rows.astype(jnp.bfloat16)


def shifted_tables(jitter, span):
    lag_index = jnp.arange(span, dtype=jnp.int32)[None, :] - jitter[:, None]
    inside = (lag_index >= 0) & (lag_index < WIN)
    clipped = jnp.clip(lag_index, 0, WIN - 1)
    bin_list = jnp.array(freq_bins, dtype=jnp.int32)
    turn_count = clipped[:, None, :] * bin_list[None, :, None] % WIN
    phase_angle = 2.0 * math.pi / WIN * turn_count.astype(jnp.float32)
    table = jnp.concatenate([jnp.cos(phase_angle), -jnp.sin(phase_angle)], axis=1) / math.sqrt(WIN)
    table = jnp.where(inside[:, None, :], table, 0.0)
    return table.astype(jnp.bfloat16)


def local_spectra(extended, sample_offsets, dft_rows):
    count_of_shots = sample_offsets.shape[0]
    reach_blocks = WIN // SPACING + 1
    jitter = sample_offsets - jnp.arange(count_of_shots, dtype=jnp.int32) * SPACING
    tables = shifted_tables(jitter, reach_blocks * SPACING)
    tables = tables.reshape(count_of_shots, dft_rows.shape[1], reach_blocks, SPACING)
    blocks = extended.reshape(extended.shape[0], extended.shape[1] // SPACING, SPACING)
    total = jnp.zeros((count_of_shots, dft_rows.shape[1], extended.shape[0]), jnp.float32)
    for offset in range(reach_blocks):
        record_part = blocks[:, offset : offset + count_of_shots, :]
        total = total + jnp.einsum(
            "rsu,scu->scr", record_part, tables[:, :, offset, :], preferred_element_type=jnp.float32
        )
    return total


def gram_terms(left, right):
    nfreq = len(freq_bins)
    left_re = left[:, :nfreq, :]
    left_im = left[:, nfreq:, :]
    right_re = right[:, :nfreq, :]
    right_im = right[:, nfreq:, :]
    gram_real = jnp.einsum("sfr,sfq->frq", left_re, right_re, preferred_element_type=jnp.float32)
    gram_real = gram_real + jnp.einsum(
        "sfr,sfq->frq", left_im, right_im, preferred_element_type=jnp.float32
    )
    gram_imag = jnp.einsum("sfr,sfq->frq", left_re, right_im, preferred_element_type=jnp.float32)
    gram_imag = gram_imag - jnp.einsum(
        "sfr,sfq->frq", left_im, right_re, preferred_element_type=jnp.float32
    )
    return jnp.stack([gram_real, gram_imag], axis=0)


def per_device(record, shot_fire_samples):
    trace_segment_length = record.shape[1]
    count_of_shots = shot_fire_samples.shape[0]
    dft_rows = dft_table(WIN)
    sample_offsets = shot_fire_samples - lax.axis_index("shot") * trace_segment_length
    head_rows = record[:, :WIN]
    rim_rows = shifted(head_rows, "shot", -1)
    extended = jnp.concatenate([record, rim_rows], axis=1)
    trace_spectra = local_spectra(extended, sample_offsets, dft_rows)
    trace_spectra = trace_spectra.astype(jnp.bfloat16)
    all_receivers = lax.all_gather(trace_spectra, "rcv", axis=2, tiled=True)
    total_shots = count_of_shots * lax.axis_size("shot")
    partial_gram = gram_terms(trace_spectra, all_receivers)
    result = lax.psum_scatter(partial_gram, "shot", scatter_dimension=3, tiled=True)
    return result / total_shots


def solution(mesh):
    return jax.shard_map(
        per_device,
        mesh=mesh,
        in_specs=(P("rcv", "shot"), P("shot")),
        out_specs=P(None, None, "rcv", "shot"),
        check_vma=False,
    )
```

profile of v0, /device:TPU:1, one launch (start us, length us, event | category | flops | bytes accessed | tf_op | source)
XLA Modules:
  0.0 363.7 jit_solution(5917377322379942619)
XLA Ops:
  6.5 1.0 slice.70
  7.6 5.1 %collective-permute-start = (bf16[96,2048]{1,0:T(8,128)(2,1)S(1)}, bf16[96,2048]{1,0:T(8,128)(2,1)S(1)}, u32[]{:S(2)}, u32[]{:S(2)}) collective-permute-start(bf16[96,2048]{1,0:T(8,128)(2,1)S(1)} %slice.70), channel_id=1, source_target_pairs={{8,0},{16,8},{24,16},{32,24},{40,32},{48,40},{56,48},{64,56},{72,6... | collective-permute-start | bytes 1179656 | tf_op jit(solution)/shard_map/ppermute | solution.py:15
  12.7 0.7 multiply_subtract_fusion
  13.5 10.4 %fusion.52 = (f32[32,4,9,256]{3,1,0,2:T(4,128)S(1)}, f32[32,4,9,256]{3,1,0,2:T(4,128)S(1)}) fusion(s32[4]{0:T(128)} %constant.43.clone, s32[32,9,256]{2,0,1:T(8,128)S(1)} %subtract_clamp_fusion), kind=kLoop, calls=%fused_computation.45 | loop fusion | flops 4423680 | bytes 2654224 | tf_op jit(solution)/shard_map/cos | solution.py:36
  24.1 0.8 fusion.1
  24.9 0.5 copy-done
  25.6 0.5 copy.78
  26.1 3.3 fusion.60
  29.5 0.9 fusion.16
  30.4 0.9 fusion.14
  31.3 0.9 fusion.12
  32.3 0.9 fusion.8
  33.2 0.9 fusion.6
  34.2 0.9 fusion.2
  35.1 1.0 fusion.31
  36.1 1.0 fusion.40
  37.1 1.0 fusion.49
  38.0 0.2 copy.58
  38.2 32.1 %all_gather.3 = bf16[32,8,768]{0,1,2:T(8,128)(2,1)S(1)} all-gather(bf16[32,8,96]{0,1,2:T(8,128)(2,1)S(1)} %copy.58), channel_id=1, replica_groups=mesh['shot'=32,'rcv'=8] {'rcv'}, dimensions={2}, use_global_device_ids=true | all-gather | bytes 442368 | tf_op jit(solution)/shard_map/all_gather | solution.py:84
  70.4 0.5 fusion.61
  70.9 0.5 copy.76
  71.4 0.5 copy.77
  71.9 0.4 fusion.58
  72.3 0.4 fusion.56
  72.6 0.4 fusion.21
  73.0 0.3 fusion.20
  73.5 2.8 copy.65
  76.4 0.6 copy-done.1
  77.0 0.6 dynamic-slice
  78.2 277.0 %all-reduce.3.cloned.1.call-done = f32[2,4,96,768]{2,1,0,3:T(4,128)} async-done(((f32[2,4,96,768]{2,1,0,3:T(4,128)}), f32[2,4,96,768]{2,1,0,3:T(4,128)}) %all-reduce.3.cloned.1.call-update) | async-done | bytes 2359312
  355.3 0.9 constant_dynamic-slice_fusion
  356.2 0.7 copy_multiply_fusion
  (11 shorter events, 0.6 us)
Async XLA Ops:
  6.5 348.7 %all-reduce.3.cloned.1.call-start = ((), (), s32[]{:S(2)}) async-start(), calls=%async_computation | async-start | bytes 6291456
  7.6 17.4 %collective-permute-start = (bf16[96,2048]{1,0:T(8,128)(2,1)S(1)}, bf16[96,2048]{1,0:T(8,128)(2,1)S(1)}, u32[]{:S(2)}, u32[]{:S(2)}) collective-permute-start(bf16[96,2048]{1,0:T(8,128)(2,1)S(1)} %slice.70), channel_id=1, source_target_pairs={{8,0},{16,8},{24,16},{32,24},{40,32},{48,40},{56,48},{64,56},{72,6... | collective-permute-start | bytes 1179656 | tf_op jit(solution)/shard_map/ppermute | solution.py:15
  24.1 1.4 copy-start
  76.3 0.7 copy-start.1
Sparse Core Ops, SparseCore 0:
  76.5 278.7 all-reduce.2
where the time goes:
time: 364 us
  waiting for transfers between devices  277 us (76%)
  blocking collectives  32.1 us (9%)
  between operations  14.2 us (4%)
  other arithmetic  13.1 us (4%)
  local copies, waits for them, and re-layouts  12 us (3%)
  matrix products  9.99 us (3%)
  starting transfers between devices  5.15 us (1%)
    unnamed x2, waiting for transfers between devices  277 us
    all_gather x1, blocking collectives, per_device(): all_receivers = lax.all_gather(trace_spectra, 'rcv', axis=2, tiled=True)  32.1 us
    cos x1, other arithmetic, shifted_tables(): jnp.cos(phase_angle)  10.4 us
    dot_general x9, matrix products, local_spectra(): jnp.einsum('rsu,scu->scr', record_part, tables[:, :, offset, :], preferre...  8.57 us
  transfers between devices with their start and end apart: 2, of which 1 were waited for; matrix products, arithmetic and copies ran while one was open for 4% of the time, Pallas kernels for 0%

commit v1 on v0

--- a/solution.py
+++ b/solution.py
@@ -81,7 +81,9 @@
     extended = jnp.concatenate([record, rim_rows], axis=1)
     trace_spectra = local_spectra(extended, sample_offsets, dft_rows)
     trace_spectra = trace_spectra.astype(jnp.bfloat16)
-    all_receivers = lax.all_gather(trace_spectra, "rcv", axis=2, tiled=True)
+    all_receivers = jnp.concatenate(
+        lax.all_to_all(jnp.stack([trace_spectra] * lax.axis_size("rcv")), "rcv", 0, 0), axis=2
+    )
     total_shots = count_of_shots * lax.axis_size("shot")
     partial_gram = gram_terms(trace_spectra, all_receivers)
     result = lax.psum_scatter(partial_gram, "shot", scatter_dimension=3, tiled=True)

time: 364 us -> 342 us (0.940)
  blocking collectives: 32.1 us -> 0 us
  waiting for transfers between devices: 277 us -> 284 us
    all_gather x1 -> x0, blocking collectives: 32.1 us -> none  [per_device(): all_receivers = lax.all_gather(trace_spectra, 'rcv', axis=2, tiled=True)]
    all_to_all x0 -> x1, waiting for transfers between devices: none -> 10.3 us  [per_device(): lax.all_to_all(jnp.stack([trace_spectra] * lax.axis_size('rcv')), 'rcv',...]
  transfers between devices with their start and end apart: 2 -> 3, of which waited for: 1 -> 2; matrix products, arithmetic and copies ran while one was open for 4% -> 4% of each run, Pallas kernels for 0% -> 0%
where the time goes in v1:
time: 342 us
  waiting for transfers between devices  284 us (83%)
  between operations  14.2 us (4%)
  other arithmetic  13.1 us (4%)
  local copies, waits for them, and re-layouts  12 us (4%)
  matrix products  9.98 us (3%)
  starting transfers between devices  8.68 us (3%)
    unnamed x2, waiting for transfers between devices  274 us
    cos x1, other arithmetic, shifted_tables(): jnp.cos(phase_angle)  10.4 us
    all_to_all x1, waiting for transfers between devices, per_device(): lax.all_to_all(jnp.stack([trace_spectra] * lax.axis_size('rcv')), 'rcv',...  10.3 us
    dot_general x9, matrix products, local_spectra(): jnp.einsum('rsu,scu->scr', record_part, tables[:, :, offset, :], preferre...  8.57 us
  transfers between devices with their start and end apart: 3, of which 2 were waited for; matrix products, arithmetic and copies ran while one was open for 4% of the time, Pallas kernels for 0%

profile of v1, /device:TPU:1, one launch (start us, length us, event | category | flops | bytes accessed | tf_op | source)
XLA Modules:
  0.0 341.8 jit_solution(15764698341918855879)
XLA Ops:
  6.5 1.0 slice.70
  7.6 5.1 %collective-permute-start = (bf16[96,2048]{1,0:T(8,128)(2,1)S(1)}, bf16[96,2048]{1,0:T(8,128)(2,1)S(1)}, u32[]{:S(2)}, u32[]{:S(2)}) collective-permute-start(bf16[96,2048]{1,0:T(8,128)(2,1)S(1)} %slice.70), channel_id=1, source_target_pairs={{8,0},{16,8},{24,16},{32,24},{40,32},{48,40},{56,48},{64,56},{72,6... | collective-permute-start | bytes 1179656 | tf_op jit(solution)/shard_map/ppermute | solution.py:15
  12.7 0.7 multiply_subtract_fusion
  13.5 10.4 %fusion.52 = (f32[32,4,9,256]{3,1,0,2:T(4,128)S(1)}, f32[32,4,9,256]{3,1,0,2:T(4,128)S(1)}) fusion(s32[4]{0:T(128)} %constant.43.clone, s32[32,9,256]{2,0,1:T(8,128)S(1)} %subtract_clamp_fusion), kind=kLoop, calls=%fused_computation.45 | loop fusion | flops 4423680 | bytes 2654224 | tf_op jit(solution)/shard_map/cos | solution.py:36
  24.1 0.8 fusion.1
  24.9 0.5 copy-done
  25.6 0.5 copy.68
  26.1 3.3 fusion.64
  29.4 0.9 fusion.16
  30.4 0.9 fusion.14
  31.3 0.9 fusion.12
  32.3 0.9 fusion.8
  33.2 0.9 fusion.6
  34.2 0.9 fusion.2
  35.1 1.0 fusion.31
  36.1 1.0 fusion.40
  37.1 1.0 fusion.49
  38.0 0.9 stack.8
  38.9 3.5 %all-to-all-start = ((bf16[8,32,8,96]{3,1,2,0:T(8,128)(2,1)}), bf16[8,32,8,96]{3,1,2,0:T(8,128)(2,1)S(1)}, u32[]{:S(2)}, u32[]{:S(2)}) async-start(bf16[8,32,8,96]{3,1,2,0:T(8,128)(2,1)} %stack.8), calls=%async_computation | async-start | bytes 1048576 | tf_op jit(solution)/shard_map/all_to_all | solution.py:85
  42.5 10.3 %all-to-all-done = bf16[8,32,8,96]{3,1,2,0:T(8,128)(2,1)S(1)} async-done(((bf16[8,32,8,96]{3,1,2,0:T(8,128)(2,1)}), bf16[8,32,8,96]{3,1,2,0:T(8,128)(2,1)S(1)}, u32[]{:S(2)}, u32[]{:S(2)}) %all-to-all-start) | async-done | bytes 393248 | tf_op jit(solution)/shard_map/all_to_all | solution.py:85
  52.8 0.3 copy.52
  53.1 0.4 reshape.68
  53.5 0.4 fusion.58
  53.9 0.3 fusion.54
  54.2 0.4 fusion.21
  54.6 0.4 fusion.20
  55.1 2.8 copy.57
  58.0 0.6 copy-done.1
  58.6 0.6 dynamic-slice
  59.9 273.5 %all-reduce.3.cloned.1.call-done = f32[2,4,96,768]{2,1,0,3:T(4,128)} async-done(((f32[2,4,96,768]{2,1,0,3:T(4,128)}), f32[2,4,96,768]{2,1,0,3:T(4,128)}) %all-reduce.3.cloned.1.call-update) | async-done | bytes 2359312
  333.4 0.9 constant_dynamic-slice_fusion
  334.3 0.7 copy_multiply_fusion
  (12 shorter events, 0.7 us)
Async XLA Ops:
  7.6 17.4 %collective-permute-start = (bf16[96,2048]{1,0:T(8,128)(2,1)S(1)}, bf16[96,2048]{1,0:T(8,128)(2,1)S(1)}, u32[]{:S(2)}, u32[]{:S(2)}) collective-permute-start(bf16[96,2048]{1,0:T(8,128)(2,1)S(1)} %slice.70), channel_id=1, source_target_pairs={{8,0},{16,8},{24,16},{32,24},{40,32},{48,40},{56,48},{64,56},{72,6... | collective-permute-start | bytes 1179656 | tf_op jit(solution)/shard_map/ppermute | solution.py:15
  24.1 1.4 copy-start
  38.9 13.8 %all-to-all-start = ((bf16[8,32,8,96]{3,1,2,0:T(8,128)(2,1)}), bf16[8,32,8,96]{3,1,2,0:T(8,128)(2,1)S(1)}, u32[]{:S(2)}, u32[]{:S(2)}) async-start(bf16[8,32,8,96]{3,1,2,0:T(8,128)(2,1)} %stack.8), calls=%async_computation | async-start | bytes 1048576 | tf_op jit(solution)/shard_map/all_to_all | solution.py:85
  42.4 290.9 %all-reduce.3.cloned.1.call-start = ((), (), s32[]{:S(2)}) async-start(), calls=%async_computation.1 | async-start | bytes 6291456
  58.0 0.7 copy-start.1
Sparse Core Ops, SparseCore 0:
  58.1 275.2 all-reduce.2
